TPU v7x, 256 devices: a whole 4x4x8 slice. The times are simulated.
256 devices in a mesh: dp: 16 (over x, y_lo, core), loop: 16 (over y_hi, z).
Axes of the slice: x: 4, y: 4 (y_hi: 2, y_lo: 2; y = y_hi * 2 + y_lo), z: 8, core: 2. Of those that a mesh axis runs over, the one named last changes fastest.
Arguments:
- tokens: bfloat16 [6144, 4096], P('dp')
- cotangent: bfloat16 [6144, 4096], P('dp'), may hold values from -6 to 6
- proj_weight: bfloat16 [4096, 4096], P(None, 'dp')
- rotation: float32 [4096, 4096], P('dp', 'loop')
- doc_lengths: int32 [96], P('dp'), may hold values from 1 to 64, as said below
Outputs:
- riemannian: float32 [4096, 4096], P('dp', 'loop')
Inputs may be any that keep to these rules, and one draw needn't show every extreme that they name: `doc_lengths`: each slot holds 1 to 64 tokens; some slot holds exactly 64 in every draw.
All inputs are finite; a program needn't handle non-finite values.
Results may differ from a plain program's by a relative error of at most 0.009.
The roundings to bfloat16 on the way count: a program that leaves them out, or rounds other values in their place, can miss the bound.
Values may be sent and summed in bfloat16 or wider, within the bound.
A program may use at most 64 MiB of HBM per device.

v0:
```python
import jax
import jax.numpy as jnp
from jax import lax
from jax.sharding import PartitionSpec as P

clip_ratio = 2.0
eps_power = 1e-06


def on_device(tokens, cotangent, proj_weight, rotation, doc_lengths):
    tok_rows, feat_width = tokens.shape
    slot_count = doc_lengths.shape[0]
    slot_len = tok_rows // slot_count
    positions = jnp.arange(tok_rows, dtype=jnp.int32)
    slot_match = (positions // slot_len)[:, None] == jnp.arange(slot_count, dtype=jnp.int32)[
        None, :
    ]
    row_lengths = jnp.sum(jnp.where(slot_match, doc_lengths[None, :], 0), axis=1)
    live_rows = positions % slot_len < row_lengths
    masked = cotangent * live_rows.astype(jnp.bfloat16)[:, None]
    block_piece = lax.all_gather(rotation.astype(jnp.bfloat16), "dp", axis=0, tiled=True)
    token_cols = tokens
    weight_rows = proj_weight
    act_sum = jnp.dot(token_cols, block_piece, preferred_element_type=jnp.float32)
    mixed_sum = lax.dot_general(
        block_piece, weight_rows, (((0,), (0,)), ((), ())), preferred_element_type=jnp.float32
    )
    row_power, col_power = lax.psum(
        (jnp.sum(act_sum * act_sum, axis=1), jnp.sum(mixed_sum * mixed_sum, axis=0)), "loop"
    )
    row_limit = clip_ratio * jnp.sqrt(row_power / feat_width + eps_power)[:, None]
    col_limit = clip_ratio * jnp.sqrt(col_power / feat_width + eps_power)[None, :]
    acts_q = jnp.clip(act_sum, -row_limit, row_limit).astype(jnp.bfloat16)
    mixed_q = jnp.clip(mixed_sum, -col_limit, col_limit).astype(jnp.bfloat16)
    grad_acts = lax.dot_general(
        masked,
        lax.all_gather(mixed_q, "dp", axis=1, tiled=True),
        (((1,), (1,)), ((), ())),
        preferred_element_type=jnp.float32,
    ).astype(jnp.bfloat16)
    cot_owned = lax.all_to_all(masked, "dp", split_axis=1, concat_axis=0, tiled=True)
    acts_every = lax.all_gather(acts_q, "dp", axis=0, tiled=True)
    grad_mixed = lax.dot_general(
        cot_owned, acts_every, (((0,), (0,)), ((), ())), preferred_element_type=jnp.float32
    ).astype(jnp.bfloat16)
    all_tokens = tok_rows * lax.axis_size("dp")
    token_cols = tokens
    weight_rows = proj_weight
    left_part = lax.dot_general(
        token_cols, grad_acts, (((0,), (0,)), ((), ())), preferred_element_type=jnp.float32
    )
    gradient = lax.psum_scatter(
        left_part + jnp.dot(weight_rows, grad_mixed, preferred_element_type=jnp.float32),
        "dp",
        scatter_dimension=0,
        tiled=True,
    ) * (1.0 / jnp.sqrt(jnp.float32(all_tokens)))
    grad_strip, rot_strip = (
        lax.all_gather(gradient, "loop", axis=1, tiled=True),
        lax.all_gather(rotation, "loop", axis=1, tiled=True),
    )
    cross = lax.psum_scatter(
        lax.dot_general(
            grad_strip,
            rotation,
            (((0,), (0,)), ((), ())),
            precision=lax.Precision.HIGHEST,
            preferred_element_type=jnp.float32,
        ),
        "dp",
        scatter_dimension=0,
        tiled=True,
    )
    correction = jnp.dot(
        rot_strip,
        lax.all_gather(cross, "dp", axis=0, tiled=True),
        precision=lax.Precision.HIGHEST,
        preferred_element_type=jnp.float32,
    )
    return gradient - correction


def solution(mesh):
    in_specs = (P("dp", None), P("dp", None), P(None, "dp"), P("dp", "loop"), P("dp"))
    out_specs = P("dp", "loop")
    return jax.shard_map(
        on_device, mesh=mesh, in_specs=in_specs, out_specs=out_specs, check_vma=False
    )
```

profile of v0, /device:TPU:1, one launch (start us, length us, event | category | flops | bytes accessed | tf_op | source)
XLA Modules:
  0.0 611.6 jit_solution(5128414571869678952)
XLA Ops:
  6.5 0.0 copy-start
  6.5 0.0 all-gather.7.cloned.1.call-start
  6.5 1.8 convert_element_type.23
  8.3 0.0 all-gather.7.cloned.1.call-update
  8.3 0.0 all-gather.9.cloned.1.call-start
  8.4 41.6 %all-gather.7.cloned.1.call-done = bf16[4096,256]{1,0:T(8,128)(2,1)} async-done(((bf16[256,256]{1,0:T(8,128)(2,1)}), bf16[4096,256]{1,0:T(8,128)(2,1)}) %all-gather.7.cloned.1.call-update) | async-done | bytes 2097168 | tf_op jit(solution)/shard_map/all_gather | solution.py:21
  50.0 3.1 multiply_reduce_fusion.1
  53.1 0.0 copy-done
  53.1 0.0 copy-done.5
  53.2 1.3 multiply_reduce_fusion
  54.5 34.8 %all-reduce = (f32[256]{0:T(256)S(1)}, f32[384]{0:T(512)S(1)}) all-reduce(f32[256]{0:T(256)S(1)} %get-tuple-element.11, f32[384]{0:T(512)S(1)} %get-tuple-element.13), channel_id=1, replica_groups=mesh['dp'=16,'loop'=16] {'loop'}, use_global_device_ids=true, to_apply=%region_2.3 | all-reduce | flops 640 | bytes 5120 | tf_op jit(solution)/shard_map/psum | solution.py:28
  89.3 0.7 minimum_convert_fusion.1
  90.0 0.0 all-gather.9.cloned.1.call-update
  90.0 0.0 all-gather.11.cloned.1.call-start
  90.1 0.7 minimum_convert_fusion
  90.8 0.0 all-gather.11.cloned.1.call-update
  90.8 0.0 copy-start.4
  90.8 0.0 reduce-scatter.3.cloned.1.call-start
  90.9 4.7 copy.11
  95.5 0.0 copy-done.4
  95.5 0.1 select_reduce_fusion
  95.6 2.2 broadcast_multiply_fusion
  97.8 0.0 copy-start.1
  97.8 54.8 %all_to_all.19 = bf16[384,16,256]{0,2,1:T(8,128)(2,1)} all-to-all(bf16[384,16,256]{0,2,1:T(8,128)(2,1)S(1)} %bitcast.23), channel_id=1, replica_groups=mesh['dp'=16,'loop'=16] {'dp'}, dimensions={1} | all-to-all | bytes 6291456 | tf_op jit(solution)/shard_map/all_to_all | solution.py:41
  152.7 0.0 copy-done.1
  152.7 4.7 copy.12
  157.3 8.4 %fusion.2 = f32[256,4096]{1,0:T(8,128)} fusion(bf16[384,4096]{1,0:T(8,128)(2,1)S(1)} %copy-done, bf16[384,4096]{0,1:T(8,128)(2,1)} %copy-done.1, bf16[256,4096]{1,0:T(8,128)(2,1)} %all-gather.9.cloned.1.call-done), kind=kOutput, calls=%fused_computation.6 | convolution fusion | flops 1610711040 | bytes 12582912 | tf_op jit(solution)/shard_map/dot_general | solution.py:49
  165.7 26.5 %all-gather.11.cloned.1.call-done = bf16[6144,256]{0,1:T(8,128)(2,1)} async-done(((bf16[384,256]{0,1:T(8,128)(2,1)}), bf16[6144,256]{0,1:T(8,128)(2,1)}) %all-gather.11.cloned.1.call-update) | async-done | bytes 3145744 | tf_op jit(solution)/shard_map/all_gather | solution.py:42
  192.3 9.4 %fusion = f32[4096,256]{0,1:T(8,128)} fusion(f32[256,4096]{1,0:T(8,128)} %fusion.2, bf16[4096,256]{1,0:T(8,128)(2,1)} %param.7, bf16[6144,256]{1,0:T(8,128)(2,1)} %bitcast.24, bf16[6144,256]{0,1:T(8,128)(2,1)} %all-gather.11.cloned.1.call-done), kind=kOutput, calls=%fused_computation.1 | convolution fusion | flops 1343291392 | bytes 16777216 | tf_op jit(solution)/shard_map/dot_general | solution.py:53
  201.7 0.0 reduce-scatter.3.cloned.1.call-update
  201.7 0.0 all-gather.13.cloned.1.call-start
  201.7 66.7 %reduce-scatter.3.cloned.1.call-done = f32[256,256]{0,1:T(8,128)} async-done(((f32[4096,256]{0,1:T(8,128)}), f32[256,256]{0,1:T(8,128)}) %reduce-scatter.3.cloned.1.call-update) | async-done | bytes 262160 | tf_op jit(solution)/shard_map/reduce_scatter | solution.py:52
  268.4 1.7 broadcast_multiply_fusion.1
  270.1 0.0 all-gather.13.cloned.1.call-update
  270.1 0.2 reduce-scatter.5.cloned.1.call-start
  270.3 99.0 %all-gather.13.cloned.1.call-done = f32[256,4096]{0,1:T(8,128)} async-done(((f32[256,256]{0,1:T(8,128)}), f32[256,4096]{0,1:T(8,128)}) %all-gather.13.cloned.1.call-update) | async-done | bytes 4194320 | tf_op jit(solution)/shard_map/all_gather | solution.py:59
  369.4 0.0 copy-done.2
  369.4 7.6 %fusion.12 = f32[4096,256]{1,0:T(8,128)} fusion(f32[256,4096]{0,1:T(8,128)} %all-gather.13.cloned.1.call-done, f32[256,256]{1,0:T(8,128)S(1)} %copy-done.2), kind=kOutput, calls=%fused_computation.31 | convolution fusion | flops 3221225472 | bytes 8650752 | tf_op jit(solution)/shard_map/dot_general | solution.py:63
  377.0 0.0 reduce-scatter.5.cloned.1.call-update
  377.0 0.0 all-gather.17.cloned.1.call-start
  377.0 0.7 all-gather.17.cloned.1.call-update
  377.8 0.0 all-gather.15.cloned.1.call-start
  377.8 66.1 %reduce-scatter.5.cloned.1.call-done = f32[256,256]{1,0:T(8,128)} async-done(((f32[4096,256]{1,0:T(8,128)}), f32[256,256]{1,0:T(8,128)}) %reduce-scatter.5.cloned.1.call-update) | async-done | bytes 262160 | tf_op jit(solution)/shard_map/reduce_scatter | solution.py:62
  443.9 0.0 all-gather.15.cloned.1.call-update
  443.9 106.0 %all-gather.17.cloned.1.call-done = f32[256,4096]{1,0:T(8,128)} async-done(((f32[256,256]{1,0:T(8,128)}), f32[256,4096]{1,0:T(8,128)}) %all-gather.17.cloned.1.call-update) | async-done | bytes 4194320 | tf_op jit(solution)/shard_map/all_gather | solution.py:60
  549.9 42.1 %all-gather.15.cloned.1.call-done = f32[4096,256]{1,0:T(8,128)} async-done(((f32[256,256]{1,0:T(8,128)}), f32[4096,256]{1,0:T(8,128)}) %all-gather.15.cloned.1.call-update) | async-done | bytes 4194320 | tf_op jit(solution)/shard_map/all_gather | solution.py:76
  592.0 10.9 %fusion.1 = f32[256,256]{0,1:T(8,128)} fusion(f32[4096,256]{1,0:T(8,128)} %all-gather.15.cloned.1.call-done, f32[256,4096]{1,0:T(8,128)} %all-gather.17.cloned.1.call-done, f32[256,256]{0,1:T(8,128)S(1)} %copy-done.3), kind=kOutput, calls=%fused_computation.5 | convolution fusion | flops 3221356544 | bytes 8912896 | tf_op jit(solution)/shard_map/dot_general | solution.py:74
  602.9 1.8 copy.13
  (9 shorter events, 0.0 us)
Async XLA Ops:
  6.5 46.6 %copy-start = (bf16[384,4096]{1,0:T(8,128)(2,1)S(1)}, bf16[384,4096]{1,0:T(8,128)(2,1)}, u32[]{:S(2)}) copy-start(bf16[384,4096]{1,0:T(8,128)(2,1)} %param.5) | copy-start | bytes 9437188
  6.5 43.5 %all-gather.7.cloned.1.call-start = ((), (), s32[]{:S(2)}) async-start(), calls=%async_computation.3 | async-start | bytes 2228224 | tf_op jit(solution)/shard_map/all_gather | solution.py:21
  8.3 149.0 %all-gather.9.cloned.1.call-start = ((), (), s32[]{:S(2)}) async-start(), calls=%async_computation.4 | async-start | bytes 2228224 | tf_op jit(solution)/shard_map/all_gather | solution.py:37
  50.0 3.2 copy-start.5
  90.0 102.2 %all-gather.11.cloned.1.call-start = ((), (), s32[]{:S(2)}) async-start(), calls=%async_computation.5 | async-start | bytes 3342336 | tf_op jit(solution)/shard_map/all_gather | solution.py:42
  90.8 4.7 copy-start.4
  90.8 177.6 %reduce-scatter.3.cloned.1.call-start = ((), (), s32[]{:S(2)}) async-start(), calls=%async_computation.6 | async-start | bytes 4456448 | tf_op jit(solution)/shard_map/reduce_scatter | solution.py:52
  97.8 54.9 %copy-start.1 = (bf16[384,4096]{0,1:T(8,128)(2,1)}, bf16[384,4096]{0,1:T(8,128)(2,1)S(1)}, u32[]{:S(2)}) copy-start(bf16[384,4096]{0,1:T(8,128)(2,1)S(1)} %broadcast_multiply_fusion) | copy-start | bytes 9437188
  201.7 167.7 %copy-start.2 = (f32[256,256]{1,0:T(8,128)S(1)}, f32[256,256]{1,0:T(8,128)}, u32[]{:S(2)}) copy-start(f32[256,256]{1,0:T(8,128)} %param.8) | copy-start | bytes 786436
  201.7 167.7 %all-gather.13.cloned.1.call-start = ((), (), s32[]{:S(2)}) async-start(), calls=%async_computation.7 | async-start | bytes 4456448 | tf_op jit(solution)/shard_map/all_gather | solution.py:59
  270.1 173.8 %reduce-scatter.5.cloned.1.call-start = ((), (), s32[]{:S(2)}) async-start(), calls=%async_computation.8 | async-start | bytes 4456448 | tf_op jit(solution)/shard_map/reduce_scatter | solution.py:62
  377.0 215.0 %copy-start.3 = (f32[256,256]{0,1:T(8,128)S(1)}, f32[256,256]{0,1:T(8,128)}, u32[]{:S(2)}) copy-start(f32[256,256]{0,1:T(8,128)} %reduce-scatter.3.cloned.1.call-done) | copy-start | bytes 786436
  377.0 172.9 %all-gather.17.cloned.1.call-start = ((), (), s32[]{:S(2)}) async-start(), calls=%async_computation.10 | async-start | bytes 4456448 | tf_op jit(solution)/shard_map/all_gather | solution.py:60
  377.8 214.3 %all-gather.15.cloned.1.call-start = ((), (), s32[]{:S(2)}) async-start(), calls=%async_computation.9 | async-start | bytes 4456448 | tf_op jit(solution)/shard_map/all_gather | solution.py:76
Sparse Core Ops, SparseCore 0:
  9.2 40.7 all-gather.6
  90.1 62.1 all-gather.8
  154.2 38.0 all-gather.10
  201.8 66.5 reduce-scatter.2
  270.9 98.4 all-gather.12
  377.1 66.7 reduce-scatter.4
  446.3 103.5 all-gather.16
  551.8 40.1 all-gather.14
where the time goes:
time: 612 us
  waiting for transfers between devices  449 us (73%)
  blocking collectives  89.7 us (15%)
  matrix products  40.7 us (7%)
  between operations  13.6 us (2%)
  local copies, waits for them, and re-layouts  11.1 us (2%)
  other arithmetic  7.14 us (1%)
    all_gather x1, waiting for transfers between devices, on_device(): lax.all_gather(rotation, 'loop', axis=1, tiled=True)  106 us
    all_gather x1, waiting for transfers between devices, on_device(): lax.all_gather(gradient, 'loop', axis=1, tiled=True)  99 us
    reduce_scatter x1, waiting for transfers between devices, on_device(): lax.psum_scatter(left_part + jnp.dot(weight_rows, grad_mixed, preferred_e...  66.7 us
    reduce_scatter x1, waiting for transfers between devices, on_device(): lax.psum_scatter(lax.dot_general(grad_strip, rotation, (((0,), (0,)), (()...  66.1 us
    all_to_all x1, blocking collectives, on_device(): lax.all_to_all(masked, 'dp', split_axis=1, concat_axis=0, tiled=True)  54.8 us
    all_gather x1, waiting for transfers between devices, on_device(): lax.all_gather(cross, 'dp', axis=0, tiled=True)  42.1 us
    all_gather x1, waiting for transfers between devices, on_device(): lax.all_gather(rotation.astype(jnp.bfloat16), 'dp', axis=0, tiled=True)  41.6 us
    psum x1, blocking collectives, on_device(): lax.psum((jnp.sum(act_sum * act_sum, axis=1), jnp.sum(mixed_sum * mixed_s...  34.8 us
  transfers between devices with their start and end apart: 8, of which 7 were waited for; matrix products, arithmetic and copies ran while one was open for 3% of the time, Pallas kernels for 0%

commit v1 on v0

v1 whole, which is shorter than its diff:
```python
import jax
import jax.numpy as jnp
from jax import lax
from jax.experimental import pallas as pl
from jax.experimental.pallas import tpu as pltpu
from jax.sharding import PartitionSpec as P

MESH = pl.DeviceIdType.MESH
BF = jnp.bfloat16
F32 = jnp.float32
CLIP_RATIO = 2.0
EPS_POWER = 1e-06
SEMS = 256


def nn(a, b):
    return lax.dot_general(a, b, (((1,), (0,)), ((), ())), preferred_element_type=F32)


def split(v):
    hi = v.astype(BF)
    return hi, (v - hi.astype(F32)).astype(BF)


def drive(*gens):
    live = list(gens)
    while live:
        for g in list(live):
            try:
                next(g)
            except StopIteration:
                live.remove(g)


def kernel(
    inv_width,
    scale,
    len_ref,
    tok_hbm,
    cot_hbm,
    w_hbm,
    rot_hbm,
    out_ref,
    xw,
    xwt,
    cot,
    rhi,
    rlo,
    mqt,
    s32,
    s_hi,
    s_lo,
    stat_mine,
    stat_all,
    gam,
    aqt,
    gat_all,
    gm_all,
    r_all,
    part_a,
    part_b,
    rc,
    rx0,
    rx1,
    ry0,
    ry1,
    ob,
    gout,
    cross,
    ssem,
    rsem,
    lsem,
):
    i = lax.axis_index("dp")
    j = lax.axis_index("loop")
    x, yl, c = i // 4, (i // 2) % 2, i % 2
    yh, z = j // 8, j % 8
    T = tok_hbm.shape[0]
    B = 256
    KB = 16

    def wrap4(v):
        return lax.rem(v + 4, 4)

    def wrap8(v):
        return lax.rem(v + 8, 8)

    xp, xm = wrap4(x + 1), wrap4(x - 1)
    x2 = wrap4(x + 2)
    XP = {"dp": xp * 4 + yl * 2 + c, "loop": j}
    XM = {"dp": xm * 4 + yl * 2 + c, "loop": j}
    YN = {"dp": x * 4 + (1 - yl) * 2 + c, "loop": j}
    CORE = {"dp": x * 4 + yl * 2 + (1 - c), "loop": j}
    zp, zm = wrap8(z + 1), wrap8(z - 1)
    ZP = {"dp": i, "loop": yh * 8 + zp}
    ZM = {"dp": i, "loop": yh * 8 + zm}
    YH = {"dp": i, "loop": (1 - yh) * 8 + z}

    def did(xx, yy, cc):
        return xx * 4 + yy * 2 + cc

    counter = [0]
    sent = []

    def send(src, dst, dev):
        k = counter[0]
        counter[0] += 1
        cp = pltpu.make_async_remote_copy(
            src_ref=src,
            dst_ref=dst,
            send_sem=ssem.at[k],
            recv_sem=rsem.at[k],
            device_id=dev,
            device_id_type=MESH,
        )
        cp.start()
        sent.append(cp)
        return cp

    def send_same(ref, dev):
        return send(ref, ref, dev)

    ld_r = pltpu.make_async_copy(rot_hbm, r_all.at[j], lsem.at[0])
    ld_x = pltpu.make_async_copy(tok_hbm, xw.at[pl.ds(0, T)], lsem.at[1])
    ld_w = pltpu.make_async_copy(w_hbm, xwt.at[:, pl.ds(T, B)], lsem.at[2])
    ld_c = pltpu.make_async_copy(cot_hbm, cot, lsem.at[3])
    ld_r.start()
    ld_w.start()
    ld_x.start()
    ld_c.start()

    barrier = pltpu.get_barrier_semaphore()
    for dev in (XP, XM, YN, CORE):
        pl.semaphore_signal(barrier, inc=1, device_id=dev, device_id_type=MESH)
    for d in range(1, 16):
        pl.semaphore_signal(
            barrier, inc=1, device_id={"dp": i, "loop": lax.rem(j + d, 16)}, device_id_type=MESH
        )
    ld_r.wait()
    rv = r_all[j]
    hv, lv = split(rv)
    own_rows = pl.ds(pl.multiple_of(i * B, B), B)
    rhi[own_rows] = hv
    rlo[own_rows] = lv
    pl.semaphore_wait(barrier, 19)

    def rows(buf, idx, part=None):
        if part is None:
            return buf.at[pl.ds(pl.multiple_of(idx * B, B), B)]
        return buf.at[pl.ds(pl.multiple_of(idx * B + part * (B // 2), B // 2), B // 2)]

    def gather_dp(buf):
        own = rows(buf, i)
        a_y = send_same(own, YN)
        a_p = send_same(own, XP)
        a_m = send_same(own, XM)
        core = [send_same(own, CORE)]
        left, right, opp = did(xm, yl, c), did(xp, yl, c), did(x2, yl, c)
        ynb = did(x, 1 - yl, c)
        yield
        a_p.wait_recv()
        r_p = send_same(rows(buf, left, 0), XP)
        y_l = send_same(rows(buf, left, 1), YN)
        core.append(send_same(rows(buf, left), CORE))
        yield
        a_m.wait_recv()
        r_m = send_same(rows(buf, right, 1), XM)
        y_r = send_same(rows(buf, right, 0), YN)
        core.append(send_same(rows(buf, right), CORE))
        yield
        a_y.wait_recv()
        d_p = send_same(rows(buf, ynb, 0), XP)
        d_m = send_same(rows(buf, ynb, 1), XM)
        core.append(send_same(rows(buf, ynb), CORE))
        yield
        r_p.wait_recv()
        y_a = send_same(rows(buf, opp, 0), YN)
        core.append(send_same(rows(buf, opp, 0), CORE))
        yield
        r_m.wait_recv()
        y_b = send_same(rows(buf, opp, 1), YN)
        core.append(send_same(rows(buf, opp, 1), CORE))
        yield
        lft2, rgt2, opp2 = did(xm, 1 - yl, c), did(xp, 1 - yl, c), did(x2, 1 - yl, c)
        for cp, ref in (
            (d_p, rows(buf, lft2, 0)),
            (d_m, rows(buf, rgt2, 1)),
            (y_l, rows(buf, lft2, 1)),
            (y_r, rows(buf, rgt2, 0)),
            (y_a, rows(buf, opp2, 0)),
            (y_b, rows(buf, opp2, 1)),
        ):
            cp.wait_recv()
            core.append(send_same(ref, CORE))
            yield
        for cp in core:
            cp.wait_recv()

    def gather_loop(buf):
        half = B // 2

        def blk(u, zz, part=None):
            ref = buf.at[u * 8 + zz]
            if part is None:
                return ref
            return ref.at[pl.ds(part * half, half)]

        own = blk(yh, z)
        oth = send_same(own, YH)
        wp = {0: send_same(own, ZP)}
        wm = {0: send_same(own, ZM)}
        lanes = (yh, 1 - yh)
        yield
        oth.wait_recv()
        wp[1] = send_same(blk(lanes[1], z), ZP)
        wm[1] = send_same(blk(lanes[1], z), ZM)
        yield
        for d in range(1, 5):
            for ln in (0, 1):
                wp[ln].wait_recv()
                if d < 4:
                    ref = blk(lanes[ln], wrap8(z - d), None if d < 3 else 0)
                    wp[ln] = send_same(ref, ZP)
                yield
                wm[ln].wait_recv()
                if d < 4:
                    ref = blk(lanes[ln], wrap8(z + d), None if d < 3 else 1)
                    wm[ln] = send_same(ref, ZM)
                yield

    def reduce_dp(k, part, chunk, out):
        rck, r0k, r1k, y0k, y1k, obk = (b.at[k] for b in (rc, rx0, rx1, ry0, ry1, ob))
        order = [(2, 0), (2, 1), (3, 0), (1, 1), (1, 0), (3, 1), (0, 0), (0, 1)]
        half, quar = B // 2, B // 4
        pend = []

        def flush(keep):
            while len(pend) > keep:
                pend.pop(0)()

        core = {}
        for d, yy in order:
            xx = wrap4(x + d)
            idx = did(xx, yy, 1 - c)
            part[idx] = chunk(idx)

            def go(idx=idx, d=d, yy=yy, xx=xx):
                core[d, yy] = send(part.at[idx], rck.at[xx * 2 + yy], CORE)

            pend.append(go)
            flush(1)
            yield
        relay, direct, yfirst = {}, {}, {}
        for d, yy in order:
            xx = wrap4(x + d)
            idx = did(xx, yy, c)
            v = chunk(idx)
            flush(0)
            core[d, yy].wait_recv()
            part[idx] = v + rck[xx * 2 + yy]
            sgn = 1 if yy == 0 else -1
            fwd, back = (XP, XM) if sgn == 1 else (XM, XP)
            if d == 2:

                def go(idx=idx, yy=yy, fwd=fwd):
                    relay[yy] = send(part.at[idx, pl.ds(0, half)], r0k.at[yy, 0], fwd)

                pend.append(go)
            elif d == (4 - sgn) % 4:

                def go(idx=idx, yy=yy, back=back):
                    direct[yy] = send(part.at[idx, pl.ds(0, half)], r0k.at[yy, 1], back)

                pend.append(go)
            if yy == 1:

                def go(d=d, xx=xx):
                    yfirst[d] = send(
                        part.at[did(xx, 1 - yl, c), pl.ds(half, half)], y1k.at[xx], YN
                    )

                if d in (2, 0):
                    pend.append(go)
            if (d, yy) == (1, 0) or (d, yy) == (3, 1):

                def go(d=d, xx=xx):
                    yfirst[d] = send(
                        part.at[did(xx, 1 - yl, c), pl.ds(half, half)], y1k.at[xx], YN
                    )

                pend.append(go)
            yield
        flush(0)

        def ring_tail(base, n, buf, item, yy, sgn, mine):
            fwd = XP if sgn == 1 else XM
            nxt = xp if sgn == 1 else xm
            ref = part.at[did(nxt, yy, c), pl.ds(base, n)]
            ref[...] = ref[...] + buf[item, 0]
            return send(ref, buf.at[item, 2], fwd)

        merged = {}
        for yy in (0, 1):
            relay[yy].wait_recv()
            merged[yy] = ring_tail(0, half, r0k, yy, yy, 1 if yy == 0 else -1, None)
            yield
        rel1, dir1, mer1 = {}, {}, {}
        for d in (2, 1, 3, 0):
            xx = wrap4(x + d)
            yfirst[d].wait_recv()
            ref = part.at[did(xx, yl, c), pl.ds(half, half)]
            ref[...] = ref[...] + y1k[xx]
            for it, sgn in ((0, 1), (1, -1)):
                fwd, back = (XP, XM) if sgn == 1 else (XM, XP)
                src = part.at[did(xx, yl, c), pl.ds(half + it * quar, quar)]
                if d == 2:
                    rel1[it] = send(src, r1k.at[it, 0], fwd)
                elif d == (4 - sgn) % 4:
                    dir1[it] = send(src, r1k.at[it, 1], back)
            yield
        for yy in (0, 1):
            direct[yy].wait_recv()
            merged[yy].wait_recv()
            obk[yy] = part[did(x, yy, c), pl.ds(0, half)] + r0k[yy, 1] + r0k[yy, 2]
        ysend = send(obk.at[1 - yl], y0k, YN)
        yield
        for it, sgn in ((0, 1), (1, -1)):
            rel1[it].wait_recv()
            mer1[it] = ring_tail(half + it * quar, quar, r1k, it, yl, sgn, None)
            yield
        ysend.wait_recv()
        out(0, half, obk[yl] + y0k[...])
        yield
        for it in (0, 1):
            dir1[it].wait_recv()
            mer1[it].wait_recv()
            base = half + it * quar
            out(base, quar, part[did(x, yl, c), pl.ds(base, quar)] + r1k[it, 1] + r1k[it, 2])
            yield

    def prepare():
        ld_w.wait()
        for g in range(4):

            @pl.loop(0, 4)
            def _(q, g=g):
                at = pl.multiple_of((g * 4 + q) * B, B)
                xw[pl.ds(T, B), pl.ds(at, B)] = xwt[pl.ds(at, B), pl.ds(T, B)].T

            yield
        ld_x.wait()
        for g in range(4):

            @pl.loop(0, 4)
            def _(q, g=g):
                at = pl.multiple_of((g * 4 + q) * B, B)
                xwt[pl.ds(at, B), pl.ds(0, T)] = xw[pl.ds(0, T), pl.ds(at, B)].T

            yield
        ld_c.wait()
        slot = T // len_ref.shape[0]
        for s in range(len_ref.shape[0]):
            keep = lax.broadcasted_iota(jnp.int32, (slot, cot.shape[1]), 0) < len_ref[s]
            cur = cot[pl.ds(s * slot, slot)].astype(F32)
            cot[pl.ds(s * slot, slot)] = jnp.where(keep, cur, 0.0).astype(BF)
            yield

    drive(gather_dp(rhi), prepare())

    KG = 1024

    def rotate(r):
        @pl.loop(0, xw.shape[1] // KG)
        def _(g):
            at = pl.multiple_of(g * KG, KG)
            s32[...] += nn(xw[:, pl.ds(at, KG)], r[pl.ds(at, KG)])

    s32[...] = jnp.zeros_like(s32)
    rotate(rhi)
    sq = s32[...]
    sq = sq * sq
    NS = s32.shape[0] // 128
    sums = jnp.sum((sq[:, :128] + sq[:, 128:]).T, axis=0, keepdims=True)
    for g in range(NS):
        stat_mine[pl.ds(g, 1)] = sums[:, g * 128 : (g + 1) * 128]
    for g in range(NS, 8):
        stat_mine[pl.ds(g, 1)] = jnp.zeros((1, 128), F32)
    stats = []
    for d in range(1, 16):
        stats.append(
            send(stat_mine, stat_all.at[d], {"dp": i, "loop": lax.rem(j + d, 16)})
        )
    for cp in stats:
        cp.wait_recv()
    power = stat_mine[...]
    for d in range(1, 16):
        power = power + stat_all[d]
    limit = CLIP_RATIO * jnp.sqrt(power * inv_width + EPS_POWER)
    for g in range(NS):
        lim = jnp.broadcast_to(limit[g : g + 1, :], (128, 128)).T
        for h in (0, 1):
            v = s32[pl.ds(g * 128, 128), pl.ds(h * 128, 128)]
            v = jnp.minimum(jnp.maximum(v, -lim), lim)
            if g * 128 < T:
                aqt[pl.ds(h * 128, 128), pl.ds(g * 128, 128)] = v.T.astype(BF)
            else:
                at = pl.multiple_of(i * B + (g * 128 - T), 128)
                mqt[pl.ds(at, 128), pl.ds(h * 128, 128)] = v.astype(BF)

    drive(gather_dp(mqt))

    ga = nn(cot[:, pl.ds(0, KG)], mqt[pl.ds(0, KG)])
    for g in range(1, 4):
        ga = ga + nn(cot[:, pl.ds(g * KG, KG)], mqt[pl.ds(g * KG, KG)])
    gam[pl.ds(0, T)] = ga.astype(BF)
    gat_all[j] = ga.T.astype(BF)

    def chunk_gm(idx):
        return nn(aqt[...], cot[:, pl.ds(pl.multiple_of(idx * B, B), B)])

    def out_gm(at, n, v):
        gm_all[j, pl.ds(at, n)] = v.astype(BF)
        gout[pl.ds(at, n)] = v

    drive(reduce_dp(0, part_a, chunk_gm, out_gm), gather_loop(gat_all), gather_loop(r_all))
    gam[pl.ds(T, B)] = gout[...].T.astype(BF)

    def chunk_g(idx):
        return nn(xwt[pl.ds(pl.multiple_of(idx * B, B), B)], gam[...])

    def out_g(at, n, v):
        gout[pl.ds(at, n)] = v * scale

    drive(gather_loop(gm_all), reduce_dp(1, part_b, chunk_g, out_g), gather_dp(rlo))
    rotate(rlo)
    sh, sl = split(s32[...])
    s_hi[...] = sh
    s_lo[...] = sl
    for cp in sent:
        cp.wait_send()
    sent.clear()

    def chunk_c(idx):
        a, b = gat_all[idx], gm_all[idx]
        return (
            nn(a, s_hi[pl.ds(0, T)])
            + nn(a, s_lo[pl.ds(0, T)])
            + nn(b, s_hi[pl.ds(T, B)])
            + nn(b, s_lo[pl.ds(T, B)])
        )

    def out_c(at, n, v):
        cross[pl.ds(pl.multiple_of(i * B + at, B // 4), n)] = v * scale

    drive(reduce_dp(2, part_a, chunk_c, out_c))
    drive(gather_dp(cross))

    @pl.loop(0, KB)
    def _(k):
        ah, al = split(r_all[k])
        bh, bl = split(cross[pl.ds(pl.multiple_of(k * B, B), B)])
        gout[...] -= nn(ah, bh) + nn(ah, bl) + nn(al, bh)

    out_ref[...] = gout[...]
    for cp in sent:
        cp.wait_send()


def solution(mesh):
    def on_device(tokens, cotangent, proj_weight, rotation, doc_lengths):
        T, D = tokens.shape
        B = rotation.shape[1]
        n = mesh.shape["dp"]
        hbm = pl.BlockSpec(memory_space=pl.ANY)
        total = T * n
        V = pltpu.VMEM

        def body(*refs):
            kernel(1.0 / D, 1.0 / (float(total) ** 0.5), *refs)

        return pl.pallas_call(
            body,
            out_shape=jax.ShapeDtypeStruct((B, B), F32),
            in_specs=[pl.BlockSpec(memory_space=pltpu.SMEM), hbm, hbm, hbm, hbm],
            out_specs=pl.BlockSpec(memory_space=pltpu.VMEM),
            scratch_shapes=[
                V((T + B, D), BF),
                V((D, T + B), BF),
                V((T, D), BF),
                V((D, B), BF),
                V((D, B), BF),
                V((D, B), BF),
                V((T + B, B), F32),
                V((T + B, B), BF),
                V((T + B, B), BF),
                V((8, 128), F32),
                V((16, 8, 128), F32),
                V((T + B, B), BF),
                V((B, T), BF),
                V((16, B, T), BF),
                V((16, B, B), BF),
                V((16, B, B), F32),
                V((16, B, B), F32),
                V((16, B, B), F32),
                V((3, 8, B, B), F32),
                V((3, 2, 3, B // 2, B), F32),
                V((3, 2, 3, B // 4, B), F32),
                V((3, B // 2, B), F32),
                V((3, 4, B // 2, B), F32),
                V((3, 2, B // 2, B), F32),
                V((B, B), F32),
                V((D, B), F32),
                pltpu.SemaphoreType.DMA((SEMS,)),
                pltpu.SemaphoreType.DMA((SEMS,)),
                pltpu.SemaphoreType.DMA((4,)),
            ],
            compiler_params=pltpu.CompilerParams(
                collective_id=0, has_side_effects=True, vmem_limit_bytes=67000000
            ),
        )(doc_lengths, tokens, cotangent, proj_weight, rotation)

    in_specs = (P("dp", None), P("dp", None), P(None, "dp"), P("dp", "loop"), P("dp"))
    return jax.shard_map(
        on_device, mesh=mesh, in_specs=in_specs, out_specs=P("dp", "loop"), check_vma=False
    )
```

time: 612 us -> 223 us (0.36)
  waiting for transfers between devices: 449 us -> 0 us
  Pallas kernels: 0 us -> 221 us
  blocking collectives: 89.7 us -> 0 us
  matrix products: 40.7 us -> 0 us
  between operations: 13.6 us -> 0.01 us
  local copies, waits for them, and re-layouts: 11.1 us -> 1.67 us
  other arithmetic: 7.14 us -> 0 us
    all_gather x6 -> x0, waiting for transfers between devices: 315 us -> none  [the longest x1 106 us: on_device(): lax.all_gather(rotation, 'loop', axis=1, tiled=True)]
    pallas_call x0 -> x1, Pallas kernels: none -> 221 us  [on_device(): pl.pallas_call(body, out_shape=jax.ShapeDtypeStruct((B, B), F32), in_spec...]
    reduce_scatter x2 -> x0, waiting for transfers between devices: 133 us -> none  [the longest x1 66.7 us: on_device(): lax.psum_scatter(left_part + jnp.dot(weight_rows, grad_mixed, preferred_e...]
    all_to_all x1 -> x0, blocking collectives: 54.8 us -> none  [on_device(): lax.all_to_all(masked, 'dp', split_axis=1, concat_axis=0, tiled=True)]
    dot_general x6 -> x0, matrix products: 40.7 us -> none  [the longest x1 10.9 us: on_device(): jnp.dot(rot_strip, lax.all_gather(cross, 'dp', axis=0, tiled=True), preci...]
    psum x1 -> x0, blocking collectives: 34.8 us -> none  [on_device(): lax.psum((jnp.sum(act_sum * act_sum, axis=1), jnp.sum(mixed_sum * mixed_s...]
  transfers between devices with their start and end apart: 8 -> 0, of which waited for: 7 -> 0; matrix products, arithmetic and copies ran while one was open for 3% -> 0% of each run, Pallas kernels for 0% -> 0%
where the time goes in v1:
time: 223 us
  Pallas kernels  221 us (99%)
    pallas_call x1, Pallas kernels, on_device(): pl.pallas_call(body, out_shape=jax.ShapeDtypeStruct((B, B), F32), in_spec...  221 us

profile of v1, /device:TPU:1, one launch (start us, length us, event | category | flops | bytes accessed | tf_op | source)
XLA Modules:
  0.0 223.1 jit_solution(1218467375629214827)
XLA Ops:
  0.0 221.4 %shard_map.55 = f32[256,256]{1,0:T(8,128)} custom-call(s32[6]{0:T(128)} %refs_0_.1, bf16[384,4096]{1,0:T(8,128)(2,1)} %refs_1_.1, bf16[384,4096]{1,0:T(8,128)(2,1)} %refs_2_.1, bf16[4096,256]{1,0:T(8,128)(2,1)} %refs_3_.1, f32[256,256]{1,0:T(8,128)} %refs_4_.1), custom_call_target="tpu_custom_call" | custom-call | tf_op jit(solution)/shard_map/pallas_call | solution.py:481
  221.5 1.7 copy.7

commit v2 on v1

--- a/solution.py
+++ b/solution.py
@@ -22,14 +22,26 @@
     return hi, (v - hi.astype(F32)).astype(BF)
 
 
-def drive(*gens):
-    live = list(gens)
+def advance(gen, steps):
+    for _ in range(steps):
+        if next(gen, StopIteration) is StopIteration:
+            return False
+    return True
+
+
+def drive(*main, beside=None):
+    live = list(main)
     while live:
-        for g in list(live):
-            try:
-                next(g)
-            except StopIteration:
-                live.remove(g)
+        for item in list(live):
+            if not advance(*item):
+                live.remove(item)
+        if beside is not None:
+            advance(*beside)
+
+
+def chain(*gens):
+    for g in gens:
+        yield from g
 
 
 def kernel(
@@ -70,6 +82,7 @@
     ssem,
     rsem,
     lsem,
+    tok,
 ):
     i = lax.axis_index("dp")
     j = lax.axis_index("loop")
@@ -130,19 +143,15 @@
     ld_c.start()
 
     barrier = pltpu.get_barrier_semaphore()
-    for dev in (XP, XM, YN, CORE):
+    for dev in (XP, XM, YN, CORE, ZP, ZM, YH):
         pl.semaphore_signal(barrier, inc=1, device_id=dev, device_id_type=MESH)
-    for d in range(1, 16):
-        pl.semaphore_signal(
-            barrier, inc=1, device_id={"dp": i, "loop": lax.rem(j + d, 16)}, device_id_type=MESH
-        )
     ld_r.wait()
     rv = r_all[j]
     hv, lv = split(rv)
     own_rows = pl.ds(pl.multiple_of(i * B, B), B)
     rhi[own_rows] = hv
     rlo[own_rows] = lv
-    pl.semaphore_wait(barrier, 19)
+    pl.semaphore_wait(barrier, 7)
 
     def rows(buf, idx, part=None):
         if part is None:
@@ -338,6 +347,16 @@
             out(base, quar, part[did(x, yl, c), pl.ds(base, quar)] + r1k[it, 1] + r1k[it, 2])
             yield
 
+    def entered():
+        for r in range(3):
+            for dev in (ZP, ZM):
+                pl.semaphore_signal(tok.at[r], inc=1, device_id=dev, device_id_type=MESH)
+            yield
+            pl.semaphore_wait(tok.at[r], 2)
+        pl.semaphore_signal(tok.at[3], inc=1, device_id=YH, device_id_type=MESH)
+        yield
+        pl.semaphore_wait(tok.at[3], 1)
+
     def prepare():
         ld_w.wait()
         for g in range(4):
@@ -365,7 +384,12 @@
             cot[pl.ds(s * slot, slot)] = jnp.where(keep, cur, 0.0).astype(BF)
             yield
 
-    drive(gather_dp(rhi), prepare())
+    ring_r = gather_loop(r_all)
+    first = gather_dp(rhi)
+    advance(first, 1)
+    advance(ring_r, 1)
+    drive((first, 1), (prepare(), 1), (entered(), 1))
+    advance(ring_r, 1)
 
     KG = 1024
 
@@ -375,8 +399,10 @@
             at = pl.multiple_of(g * KG, KG)
             s32[...] += nn(xw[:, pl.ds(at, KG)], r[pl.ds(at, KG)])
 
+        yield
+
     s32[...] = jnp.zeros_like(s32)
-    rotate(rhi)
+    drive((rotate(rhi), 1))
     sq = s32[...]
     sq = sq * sq
     NS = s32.shape[0] // 128
@@ -407,7 +433,8 @@
                 at = pl.multiple_of(i * B + (g * 128 - T), 128)
                 mqt[pl.ds(at, 128), pl.ds(h * 128, 128)] = v.astype(BF)
 
-    drive(gather_dp(mqt))
+    advance(ring_r, 4)
+    drive((gather_dp(mqt), 1))
 
     ga = nn(cot[:, pl.ds(0, KG)], mqt[pl.ds(0, KG)])
     for g in range(1, 4):
@@ -422,7 +449,10 @@
         gm_all[j, pl.ds(at, n)] = v.astype(BF)
         gout[pl.ds(at, n)] = v
 
-    drive(reduce_dp(0, part_a, chunk_gm, out_gm), gather_loop(gat_all), gather_loop(r_all))
+    ring_ga, ring_gm = gather_loop(gat_all), gather_loop(gm_all)
+    advance(ring_ga, 1)
+    drive((reduce_dp(0, part_a, chunk_gm, out_gm), 3), beside=(ring_ga, 1))
+    advance(ring_gm, 1)
     gam[pl.ds(T, B)] = gout[...].T.astype(BF)
 
     def chunk_g(idx):
@@ -431,8 +461,9 @@
     def out_g(at, n, v):
         gout[pl.ds(at, n)] = v * scale
 
-    drive(gather_loop(gm_all), reduce_dp(1, part_b, chunk_g, out_g), gather_dp(rlo))
-    rotate(rlo)
+    rings = chain(ring_ga, ring_gm)
+    drive((reduce_dp(1, part_b, chunk_g, out_g), 3), beside=(rings, 1))
+    drive((chain(gather_dp(rlo), rotate(rlo)), 1), (rings, 1))
     sh, sl = split(s32[...])
     s_hi[...] = sh
     s_lo[...] = sl
@@ -452,8 +483,8 @@
     def out_c(at, n, v):
         cross[pl.ds(pl.multiple_of(i * B + at, B // 4), n)] = v * scale
 
-    drive(reduce_dp(2, part_a, chunk_c, out_c))
-    drive(gather_dp(cross))
+    drive((reduce_dp(2, part_a, chunk_c, out_c), 3), beside=(ring_r, 1))
+    drive((gather_dp(cross), 2), (ring_r, 1))
 
     @pl.loop(0, KB)
     def _(k):
@@ -513,6 +544,7 @@
                 pltpu.SemaphoreType.DMA((SEMS,)),
                 pltpu.SemaphoreType.DMA((SEMS,)),
                 pltpu.SemaphoreType.DMA((4,)),
+                pltpu.SemaphoreType.REGULAR((4,)),
             ],
             compiler_params=pltpu.CompilerParams(
                 collective_id=0, has_side_effects=True, vmem_limit_bytes=67000000

time: 223 us -> 177 us (0.79)
  Pallas kernels: 221 us -> 175 us
    pallas_call x1, Pallas kernels: 221 us -> 175 us  [on_device(): pl.pallas_call(body, out_shape=jax.ShapeDtypeStruct((B, B), F32), in_spec...]
where the time goes in v2:
time: 177 us
  Pallas kernels  175 us (99%)
    pallas_call x1, Pallas kernels, on_device(): pl.pallas_call(body, out_shape=jax.ShapeDtypeStruct((B, B), F32), in_spec...  175 us

profile of v2, /device:TPU:1, one launch (start us, length us, event | category | flops | bytes accessed | tf_op | source)
XLA Modules:
  0.0 176.8 jit_solution(15541889011359658157)
XLA Ops:
  0.0 175.1 %shard_map.55 = f32[256,256]{1,0:T(8,128)} custom-call(s32[6]{0:T(128)} %refs_0_.1, bf16[384,4096]{1,0:T(8,128)(2,1)} %refs_1_.1, bf16[384,4096]{1,0:T(8,128)(2,1)} %refs_2_.1, bf16[4096,256]{1,0:T(8,128)(2,1)} %refs_3_.1, f32[256,256]{1,0:T(8,128)} %refs_4_.1), custom_call_target="tpu_custom_call" | custom-call | tf_op jit(solution)/shard_map/pallas_call | solution.py:512
  175.1 1.7 copy.7

commit v3 on v2

--- a/solution.py
+++ b/solution.py
@@ -83,6 +83,7 @@
     rsem,
     lsem,
     tok,
+    ga32,
 ):
     i = lax.axis_index("dp")
     j = lax.axis_index("loop")
@@ -90,7 +91,6 @@
     yh, z = j // 8, j % 8
     T = tok_hbm.shape[0]
     B = 256
-    KB = 16
 
     def wrap4(v):
         return lax.rem(v + 4, 4)
@@ -158,52 +158,81 @@
             return buf.at[pl.ds(pl.multiple_of(idx * B, B), B)]
         return buf.at[pl.ds(pl.multiple_of(idx * B + part * (B // 2), B // 2), B // 2)]
 
-    def gather_dp(buf):
-        own = rows(buf, i)
-        a_y = send_same(own, YN)
-        a_p = send_same(own, XP)
-        a_m = send_same(own, XM)
-        core = [send_same(own, CORE)]
+    def gather_dp(buf, use):
         left, right, opp = did(xm, yl, c), did(xp, yl, c), did(x2, yl, c)
         ynb = did(x, 1 - yl, c)
-        yield
-        a_p.wait_recv()
+        lft2, rgt2, opp2 = did(xm, 1 - yl, c), did(xp, 1 - yl, c), did(x2, 1 - yl, c)
+        core = []
+
+        def pair(ref, xx=None, yy=None):
+            core.append((send_same(ref, CORE), None if xx is None else did(xx, yy, 1 - c)))
+
+        def meet(n):
+            for _ in range(n):
+                cp, idx = core.pop(0)
+                cp.wait_recv()
+                if idx is not None:
+                    use(idx)
+
+        a_y0 = send_same(rows(buf, i, 0), YN)
+        a_p0 = send_same(rows(buf, i, 0), XP)
+        a_m1 = send_same(rows(buf, i, 1), XM)
+        a_y1 = send_same(rows(buf, i, 1), YN)
+        a_p1 = send_same(rows(buf, i, 1), XP)
+        a_m0 = send_same(rows(buf, i, 0), XM)
+        pair(rows(buf, i), x, yl)
+        yield
+        use(i)
+        a_p0.wait_recv()
         r_p = send_same(rows(buf, left, 0), XP)
+        a_m1.wait_recv()
+        r_m = send_same(rows(buf, right, 1), XM)
+        yield
+        a_y0.wait_recv()
+        d_p = send_same(rows(buf, ynb, 0), XP)
+        a_y1.wait_recv()
+        d_m = send_same(rows(buf, ynb, 1), XM)
+        yield
+        a_p1.wait_recv()
         y_l = send_same(rows(buf, left, 1), YN)
-        core.append(send_same(rows(buf, left), CORE))
-        yield
-        a_m.wait_recv()
-        r_m = send_same(rows(buf, right, 1), XM)
+        pair(rows(buf, left), xm, yl)
+        a_m0.wait_recv()
         y_r = send_same(rows(buf, right, 0), YN)
-        core.append(send_same(rows(buf, right), CORE))
-        yield
-        a_y.wait_recv()
-        d_p = send_same(rows(buf, ynb, 0), XP)
-        d_m = send_same(rows(buf, ynb, 1), XM)
-        core.append(send_same(rows(buf, ynb), CORE))
+        pair(rows(buf, right), xp, yl)
+        pair(rows(buf, ynb), x, 1 - yl)
+        use(left)
         yield
         r_p.wait_recv()
         y_a = send_same(rows(buf, opp, 0), YN)
-        core.append(send_same(rows(buf, opp, 0), CORE))
-        yield
         r_m.wait_recv()
         y_b = send_same(rows(buf, opp, 1), YN)
-        core.append(send_same(rows(buf, opp, 1), CORE))
-        yield
-        lft2, rgt2, opp2 = did(xm, 1 - yl, c), did(xp, 1 - yl, c), did(x2, 1 - yl, c)
-        for cp, ref in (
-            (d_p, rows(buf, lft2, 0)),
-            (d_m, rows(buf, rgt2, 1)),
-            (y_l, rows(buf, lft2, 1)),
-            (y_r, rows(buf, rgt2, 0)),
-            (y_a, rows(buf, opp2, 0)),
-            (y_b, rows(buf, opp2, 1)),
-        ):
-            cp.wait_recv()
-            core.append(send_same(ref, CORE))
-            yield
-        for cp in core:
-            cp.wait_recv()
+        pair(rows(buf, opp), x2, yl)
+        use(right)
+        use(ynb)
+        meet(1)
+        yield
+        use(opp)
+        meet(1)
+        yield
+        d_p.wait_recv()
+        y_l.wait_recv()
+        pair(rows(buf, lft2), xm, 1 - yl)
+        use(lft2)
+        yield
+        d_m.wait_recv()
+        y_r.wait_recv()
+        pair(rows(buf, rgt2), xp, 1 - yl)
+        use(rgt2)
+        meet(2)
+        yield
+        y_a.wait_recv()
+        pair(rows(buf, opp2, 0))
+        meet(1)
+        yield
+        y_b.wait_recv()
+        pair(rows(buf, opp2, 1), x2, 1 - yl)
+        use(opp2)
+        meet(len(core))
 
     def gather_loop(buf):
         half = B // 2
@@ -357,7 +386,7 @@
         yield
         pl.semaphore_wait(tok.at[3], 1)
 
-    def prepare():
+    def flip_w():
         ld_w.wait()
         for g in range(4):
 
@@ -368,6 +397,8 @@
 
             yield
         ld_x.wait()
+
+    def flip_x():
         for g in range(4):
 
             @pl.loop(0, 4)
@@ -376,6 +407,8 @@
                 xwt[pl.ds(at, B), pl.ds(0, T)] = xw[pl.ds(0, T), pl.ds(at, B)].T
 
             yield
+
+    def mask():
         ld_c.wait()
         slot = T // len_ref.shape[0]
         for s in range(len_ref.shape[0]):
@@ -384,25 +417,33 @@
             cot[pl.ds(s * slot, slot)] = jnp.where(keep, cur, 0.0).astype(BF)
             yield
 
+    def cols(idx):
+        return pl.ds(pl.multiple_of(idx * B, B), B)
+
+    def rotate(r):
+        def use(idx):
+            s32[...] += nn(xw[:, cols(idx)], r[cols(idx)])
+
+        return use
+
+    s32[...] = jnp.zeros_like(s32)
+    ga32[...] = jnp.zeros_like(ga32)
     ring_r = gather_loop(r_all)
-    first = gather_dp(rhi)
+    first, hello = gather_dp(rhi, rotate(rhi)), entered()
     advance(first, 1)
     advance(ring_r, 1)
-    drive((first, 1), (prepare(), 1), (entered(), 1))
+    advance(hello, 1)
+    drive((flip_w(), 1))
+    advance(first, 1)
+    advance(hello, 1)
+    advance(first, 1)
     advance(ring_r, 1)
-
-    KG = 1024
-
-    def rotate(r):
-        @pl.loop(0, xw.shape[1] // KG)
-        def _(g):
-            at = pl.multiple_of(g * KG, KG)
-            s32[...] += nn(xw[:, pl.ds(at, KG)], r[pl.ds(at, KG)])
-
-        yield
-
-    s32[...] = jnp.zeros_like(s32)
-    drive((rotate(rhi), 1))
+    advance(first, 1)
+    advance(hello, 1)
+    advance(first, 2)
+    advance(hello, 1)
+    drive((first, 1))
+    drive((hello, 1))
     sq = s32[...]
     sq = sq * sq
     NS = s32.shape[0] // 128
@@ -416,6 +457,7 @@
         stats.append(
             send(stat_mine, stat_all.at[d], {"dp": i, "loop": lax.rem(j + d, 16)})
         )
+    drive((flip_x(), 1), (mask(), 1))
     for cp in stats:
         cp.wait_recv()
     power = stat_mine[...]
@@ -434,11 +476,12 @@
                 mqt[pl.ds(at, 128), pl.ds(h * 128, 128)] = v.astype(BF)
 
     advance(ring_r, 4)
-    drive((gather_dp(mqt), 1))
-
-    ga = nn(cot[:, pl.ds(0, KG)], mqt[pl.ds(0, KG)])
-    for g in range(1, 4):
-        ga = ga + nn(cot[:, pl.ds(g * KG, KG)], mqt[pl.ds(g * KG, KG)])
+
+    def back(idx):
+        ga32[...] += nn(cot[:, cols(idx)], mqt[cols(idx)])
+
+    drive((gather_dp(mqt, back), 1))
+    ga = ga32[...]
     gam[pl.ds(0, T)] = ga.astype(BF)
     gat_all[j] = ga.T.astype(BF)
 
@@ -463,7 +506,7 @@
 
     rings = chain(ring_ga, ring_gm)
     drive((reduce_dp(1, part_b, chunk_g, out_g), 3), beside=(rings, 1))
-    drive((chain(gather_dp(rlo), rotate(rlo)), 1), (rings, 1))
+    drive((gather_dp(rlo, rotate(rlo)), 1), (rings, 1))
     sh, sl = split(s32[...])
     s_hi[...] = sh
     s_lo[...] = sl
@@ -484,14 +527,16 @@
         cross[pl.ds(pl.multiple_of(i * B + at, B // 4), n)] = v * scale
 
     drive((reduce_dp(2, part_a, chunk_c, out_c), 3), beside=(ring_r, 1))
-    drive((gather_dp(cross), 2), (ring_r, 1))
-
-    @pl.loop(0, KB)
-    def _(k):
-        ah, al = split(r_all[k])
-        bh, bl = split(cross[pl.ds(pl.multiple_of(k * B, B), B)])
+
+    def correct(idx):
+        ah, al = split(r_all[idx])
+        bh, bl = split(cross[cols(idx)])
         gout[...] -= nn(ah, bh) + nn(ah, bl) + nn(al, bh)
 
+    last = gather_dp(cross, correct)
+    advance(last, 1)
+    drive((ring_r, 1))
+    drive((last, 1))
     out_ref[...] = gout[...]
     for cp in sent:
         cp.wait_send()
@@ -545,6 +590,7 @@
                 pltpu.SemaphoreType.DMA((SEMS,)),
                 pltpu.SemaphoreType.DMA((4,)),
                 pltpu.SemaphoreType.REGULAR((4,)),
+                V((T, B), F32),
             ],
             compiler_params=pltpu.CompilerParams(
                 collective_id=0, has_side_effects=True, vmem_limit_bytes=67000000

time: 177 us -> 167 us (0.944)
  Pallas kernels: 175 us -> 166 us
    pallas_call x1, Pallas kernels: 175 us -> 166 us  [on_device(): pl.pallas_call(body, out_shape=jax.ShapeDtypeStruct((B, B), F32), in_spec...]
where the time goes in v3:
time: 167 us
  Pallas kernels  166 us (99%)
  local copies, waits for them, and re-layouts  1.67 us (1%)
    pallas_call x1, Pallas kernels, on_device(): pl.pallas_call(body, out_shape=jax.ShapeDtypeStruct((B, B), F32), in_spec...  166 us

profile of v3, /device:TPU:1, one launch (start us, length us, event | category | flops | bytes accessed | tf_op | source)
XLA Modules:
  0.0 167.2 jit_solution(11840029018412744379)
XLA Ops:
  0.0 165.5 %shard_map.55 = f32[256,256]{1,0:T(8,128)} custom-call(s32[6]{0:T(128)} %refs_0_.1, bf16[384,4096]{1,0:T(8,128)(2,1)} %refs_1_.1, bf16[384,4096]{1,0:T(8,128)(2,1)} %refs_2_.1, bf16[4096,256]{1,0:T(8,128)(2,1)} %refs_3_.1, f32[256,256]{1,0:T(8,128)} %refs_4_.1), custom_call_target="tpu_custom_call" | custom-call | tf_op jit(solution)/shard_map/pallas_call | solution.py:557
  165.6 1.7 copy.7

commit v4 on v3

--- a/solution.py
+++ b/solution.py
@@ -84,6 +84,7 @@
     lsem,
     tok,
     ga32,
+    lim_all,
 ):
     i = lax.axis_index("dp")
     j = lax.axis_index("loop")
@@ -444,6 +445,24 @@
     advance(hello, 1)
     drive((first, 1))
     drive((hello, 1))
+    mqt[own_rows] = s32[pl.ds(T, B)].astype(BF)
+    queue, limits_here = [], []
+
+    def back(idx):
+        if not limits_here:
+            queue.append(idx)
+            return
+        halves = []
+        for g in (0, 1):
+            lim = lim_all[idx, pl.ds(T // 128 + g, 1)]
+            lim = jnp.broadcast_to(lim, (128, 128)).T.astype(BF).astype(F32)
+            at = pl.multiple_of(idx * B + g * 128, 128)
+            row = [mqt[pl.ds(at, 128), pl.ds(h * 128, 128)].astype(F32) for h in (0, 1)]
+            row = [jnp.minimum(jnp.maximum(v, -lim), lim).astype(BF) for v in row]
+            halves.append(jnp.concatenate(row, axis=1))
+        ga32[...] += nn(cot[:, cols(idx)], jnp.concatenate(halves, axis=0))
+
+    mixing = gather_dp(mqt, back)
     sq = s32[...]
     sq = sq * sq
     NS = s32.shape[0] // 128
@@ -452,11 +471,13 @@
         stat_mine[pl.ds(g, 1)] = sums[:, g * 128 : (g + 1) * 128]
     for g in range(NS, 8):
         stat_mine[pl.ds(g, 1)] = jnp.zeros((1, 128), F32)
+    advance(mixing, 1)
     stats = []
     for d in range(1, 16):
         stats.append(
             send(stat_mine, stat_all.at[d], {"dp": i, "loop": lax.rem(j + d, 16)})
         )
+    advance(mixing, 2)
     drive((flip_x(), 1), (mask(), 1))
     for cp in stats:
         cp.wait_recv()
@@ -464,23 +485,25 @@
     for d in range(1, 16):
         power = power + stat_all[d]
     limit = CLIP_RATIO * jnp.sqrt(power * inv_width + EPS_POWER)
-    for g in range(NS):
+    lim_all[i] = limit
+    for g in range(T // 128):
         lim = jnp.broadcast_to(limit[g : g + 1, :], (128, 128)).T
         for h in (0, 1):
             v = s32[pl.ds(g * 128, 128), pl.ds(h * 128, 128)]
             v = jnp.minimum(jnp.maximum(v, -lim), lim)
-            if g * 128 < T:
-                aqt[pl.ds(h * 128, 128), pl.ds(g * 128, 128)] = v.T.astype(BF)
-            else:
-                at = pl.multiple_of(i * B + (g * 128 - T), 128)
-                mqt[pl.ds(at, 128), pl.ds(h * 128, 128)] = v.astype(BF)
-
+            aqt[pl.ds(h * 128, 128), pl.ds(g * 128, 128)] = v.T.astype(BF)
+    told = []
+    for d in range(1, 16):
+        dev = {"dp": lax.rem(i + d, 16), "loop": j}
+        told.append(send_same(lim_all.at[i], dev))
+    advance(mixing, 2)
     advance(ring_r, 4)
-
-    def back(idx):
-        ga32[...] += nn(cot[:, cols(idx)], mqt[cols(idx)])
-
-    drive((gather_dp(mqt, back), 1))
+    for cp in told:
+        cp.wait_recv()
+    limits_here.append(True)
+    for idx in queue:
+        back(idx)
+    drive((mixing, 1))
     ga = ga32[...]
     gam[pl.ds(0, T)] = ga.astype(BF)
     gat_all[j] = ga.T.astype(BF)
@@ -591,6 +614,7 @@
                 pltpu.SemaphoreType.DMA((4,)),
                 pltpu.SemaphoreType.REGULAR((4,)),
                 V((T, B), F32),
+                V((16, 8, 128), F32),
             ],
             compiler_params=pltpu.CompilerParams(
                 collective_id=0, has_side_effects=True, vmem_limit_bytes=67000000

time: 167 us -> 167 us (level)
  no operation moved by 1% of the time
where the time goes in v4:
time: 167 us; the launch traced here: 166 us
  Pallas kernels  165 us (99%)
  local copies, waits for them, and re-layouts  1.67 us (1%)
    pallas_call x1, Pallas kernels, on_device(): pl.pallas_call(body, out_shape=jax.ShapeDtypeStruct((B, B), F32), in_spec...  165 us

profile of v4, /device:TPU:1, one launch (start us, length us, event | category | flops | bytes accessed | tf_op | source)
XLA Modules:
  0.0 166.5 jit_solution(3405943699096695948)
XLA Ops:
  0.0 164.8 %shard_map.55 = f32[256,256]{1,0:T(8,128)} custom-call(s32[6]{0:T(128)} %refs_0_.1, bf16[384,4096]{1,0:T(8,128)(2,1)} %refs_1_.1, bf16[384,4096]{1,0:T(8,128)(2,1)} %refs_2_.1, bf16[4096,256]{1,0:T(8,128)(2,1)} %refs_3_.1, f32[256,256]{1,0:T(8,128)} %refs_4_.1), custom_call_target="tpu_custom_call" | custom-call | tf_op jit(solution)/shard_map/pallas_call | solution.py:580
  164.8 1.7 %copy.7 = f32[256,256]{1,0:T(8,128)} copy(f32[256,256]{1,0:T(8,128)} %shard_map.55) | data formatting | bytes 524288

commit v5 on v4

--- a/solution.py
+++ b/solution.py
@@ -549,7 +549,7 @@
     def out_c(at, n, v):
         cross[pl.ds(pl.multiple_of(i * B + at, B // 4), n)] = v * scale
 
-    drive((reduce_dp(2, part_a, chunk_c, out_c), 3), beside=(ring_r, 1))
+    drive((reduce_dp(2, part_a, chunk_c, out_c), 4), beside=(ring_r, 1))
 
     def correct(idx):
         ah, al = split(r_all[idx])

time: 167 us -> 167 us (level)
  no operation moved by 1% of the time
where the time goes in v5:
time: 167 us
  Pallas kernels  165 us (99%)
  local copies, waits for them, and re-layouts  1.67 us (1%)
    pallas_call x1, Pallas kernels, on_device(): pl.pallas_call(body, out_shape=jax.ShapeDtypeStruct((B, B), F32), in_spec...  165 us

profile of v5, /device:TPU:1, one launch (start us, length us, event | category | flops | bytes accessed | tf_op | source)
XLA Modules:
  0.0 166.6 jit_solution(3936875409827719795)
XLA Ops:
  0.0 164.9 %shard_map.55 = f32[256,256]{1,0:T(8,128)} custom-call(s32[6]{0:T(128)} %refs_0_.1, bf16[384,4096]{1,0:T(8,128)(2,1)} %refs_1_.1, bf16[384,4096]{1,0:T(8,128)(2,1)} %refs_2_.1, bf16[4096,256]{1,0:T(8,128)(2,1)} %refs_3_.1, f32[256,256]{1,0:T(8,128)} %refs_4_.1), custom_call_target="tpu_custom_call" | custom-call | tf_op jit(solution)/shard_map/pallas_call | solution.py:580
  164.9 1.7 %copy.7 = f32[256,256]{1,0:T(8,128)} copy(f32[256,256]{1,0:T(8,128)} %shard_map.55) | data formatting | bytes 524288
